TPU v7x, 32 devices: a whole 2x2x4 slice. The times are simulated.
32 devices in a mesh: domain: 8 (over z, y), vec: 4 (over x, core).
Axes of the slice: x: 2, y: 2, z: 4, core: 2. Of those that a mesh axis runs over, the one named last changes fastest.
Arguments:
- vectors: float32 [4096, 512], P('domain', 'vec'), may hold values from -6 to 6
- hamiltonian: float32 [512, 128, 128], P('domain'), may hold values from -0.09375 to 0.09375
- tile_pairs: int32 [512, 2], P('domain'), may hold values from 0 to 31, as said below
- tile_counts: int32 [8], P('domain'), may hold values from 8 to 64, as said below
Outputs:
- filtered: float32 [4096, 512], P('domain', 'vec')
- gram: float32 [512, 512], P('vec')
Inputs may be any that keep to these rules, and one draw needn't show every extreme that they name: `tile_pairs`: slots k * 64 to (k + 1) * 64 - 1 have their row group r among groups k * 4 to (k + 1) * 4 - 1 and their column group c with r <= c <= min(k * 4 + 3 * 4 - 1, 31); pairs may repeat, and repeated blocks add. `tile_counts`: one domain index uses all 64 slots.
All inputs are finite; a program needn't handle non-finite values.
Results may differ from a plain program's by a relative error of at most 0.0003.
Values sent between devices are 32-bit elements; how exact they have to be, the bound alone decides.
A program may use at most 64 MiB of HBM per device.

v0:
```python
import jax
import jax.numpy as jnp
from jax import lax
from jax.sharding import PartitionSpec as P

TILE = 128
REACH = 2
center_shift = 1.0
half_width = 1.5


def from_behind(block, axis, distance):
    devices = range(lax.axis_size(axis))
    route = [(i - distance, i) for i in devices if i - distance in devices]
    return lax.ppermute(block, axis, route)


def local_products(own, window, tiles, row_loc, col_loc, count, groups):
    block_slots = 8
    width = own.shape[2]
    span = window.shape[0]
    n_blocks = (count + block_slots - 1) // block_slots

    def block_step(index, carry):
        rows_acc, back_acc = carry
        start = index * block_slots
        tile = lax.dynamic_slice_in_dim(tiles, start, block_slots, 0)
        rloc = lax.dynamic_slice_in_dim(row_loc, start, block_slots, 0)
        cloc = lax.dynamic_slice_in_dim(col_loc, start, block_slots, 0)
        used = (start + jnp.arange(block_slots, dtype=jnp.int32) < count).astype(jnp.float32)
        apart = (rloc != cloc).astype(jnp.float32)
        fwd = jnp.einsum("tij,tjc->tic", tile, window[cloc], precision=lax.Precision.HIGHEST)
        back = jnp.einsum("tji,tjc->tic", tile, own[rloc], precision=lax.Precision.HIGHEST)
        row_hot = (rloc[:, None] == jnp.arange(groups, dtype=jnp.int32)[None, :]).astype(
            jnp.float32
        ) * used[:, None]
        col_hot = (cloc[:, None] == jnp.arange(span, dtype=jnp.int32)[None, :]).astype(
            jnp.float32
        ) * (used * apart)[:, None]
        rows_acc = rows_acc + jnp.einsum(
            "tg,tic->gic", row_hot, fwd, precision=lax.Precision.HIGHEST
        )
        back_acc = back_acc + jnp.einsum(
            "tg,tic->gic", col_hot, back, precision=lax.Precision.HIGHEST
        )
        return (rows_acc, back_acc)

    start_rows = jnp.zeros((groups, TILE, width), jnp.float32)
    start_back = jnp.zeros((span, TILE, width), jnp.float32)
    return lax.fori_loop(0, n_blocks, block_step, (start_rows, start_back))


def apply_ham(block, tiles, row_loc, col_loc, count):
    groups = block.shape[0] // TILE
    width = block.shape[1]
    own = block.reshape(groups, TILE, width)
    pieces = [own]
    for step in range(1, REACH + 1):
        pieces.append(from_behind(own, "domain", -step))
    window = jnp.concatenate(pieces, 0)
    rows_acc, back_acc = local_products(own, window, tiles, row_loc, col_loc, count, groups)
    result = rows_acc + back_acc[:groups]
    for step in range(1, REACH + 1):
        result = result + from_behind(back_acc[step * groups : (step + 1) * groups], "domain", step)
    return result.reshape(groups * TILE, width)


def shards(vectors, hamiltonian, tile_pairs, tile_counts):
    groups = vectors.shape[0] // TILE
    base = lax.axis_index("domain") * groups
    count = tile_counts[0]
    diag = tile_pairs[:, 0] == tile_pairs[:, 1]
    tiles = jnp.where(
        diag[:, None, None], 0.5 * (hamiltonian + jnp.swapaxes(hamiltonian, 1, 2)), hamiltonian
    )
    row_loc = tile_pairs[:, 0] - base
    col_loc = tile_pairs[:, 1] - base
    second = (
        apply_ham(vectors, tiles, row_loc, col_loc, count) - center_shift * vectors
    ) / half_width
    third = (
        2.0
        * (apply_ham(second, tiles, row_loc, col_loc, count) - center_shift * second)
        / half_width
        - vectors
    )
    filtered = (
        2.0 * (apply_ham(third, tiles, row_loc, col_loc, count) - center_shift * third) / half_width
        - second
    )
    total_rows = vectors.shape[0] * lax.axis_size("domain")
    gathered = lax.all_gather(filtered, "vec", axis=1, tiled=True)
    partial_block = (
        jnp.dot(
            filtered.T,
            gathered,
            precision=lax.Precision.HIGHEST,
            preferred_element_type=jnp.float32,
        )
        / total_rows
    )
    gram = lax.psum(partial_block, "domain")
    return (filtered, gram)


def solution(mesh):
    in_specs = (P("domain", "vec"), P("domain", None, None), P("domain", None), P("domain"))
    out_specs = (P("domain", "vec"), P("vec", None))
    return jax.shard_map(shards, mesh=mesh, in_specs=in_specs, out_specs=out_specs, check_vma=False)
```

profile of v0, /device:TPU:0, one launch (start us, length us, event | category | flops | bytes accessed | tf_op | source)
XLA Modules:
  0.0 392.4 jit_solution(13187985193437510828)
XLA Ops:
  9.8 5.6 %copy.6 = f32[64,128,128]{1,2,0:T(8,128)} copy(f32[64,128,128]{2,1,0:T(8,128)} %param.11) | data formatting | bytes 8388608 | tf_op args[1]
  15.4 5.9 %fusion.61 = f32[64,128,128]{2,1,0:T(8,128)} fusion(f32[64,128,128]{2,1,0:T(8,128)} %param.11, f32[64,128,128]{1,2,0:T(8,128)} %copy.6, pred[64]{0:T(512)(128)(4,1)S(1)} %compare_bitcast_fusion), kind=kLoop, calls=%fused_computation.98 | loop fusion | flops 3145728 | bytes 12582976 | tf_op jit(solution)/shard_map/jit(_where)/select_n | solution.py:73
  22.3 24.5 %while.36 = (s32[]{:T(128)}, f32[4,128,128]{2,0,1:T(4,128)S(1)}, f32[12,128,128]{2,0,1:T(8,128)S(1)}, s32[]{:T(128)}, s32[64]{0:T(128)S(1)}, /*index=5*/s32[]{:T...) while((s32[]{:T(128)}, f32[4,128,128]{2,0,1:T(4,128)S(1)}, ...), condition=%wide.region_1.2_spmd, body=%wide.region_0.1_spmd.sunk | while | flops 428083552 | bytes 8397583 | solution.py:50
  23.6 1.7 fusion.116
  26.9 2.1 fusion.117
  29.0 1.5 convolution_add_fusion.13
  31.8 1.7 fusion.116
  35.1 2.1 fusion.117
  37.1 1.5 convolution_add_fusion.13
  40.0 1.7 fusion.116
  43.2 2.1 fusion.117
  45.3 1.5 convolution_add_fusion.13
  46.9 1.3 collective-permute-start.3
  48.2 5.6 %collective-permute-start.2 = (f32[4,128,128]{2,0,1:T(4,128)S(1)}, f32[4,128,128]{2,0,1:T(4,128)S(1)}, u32[]{:S(2)}, u32[]{:S(2)}) collective-permute-start(f32[4,128,128]{2,0,1:T(4,128)S(1)} %get-tuple-element.252), channel_id=1, source_target_pairs={{0,4},{4,8},{8,12},{12,16},{16,20},{20,24},{24,28},{1,5},{5,9},{9,... | collective-permute-start | bytes 786440 | tf_op jit(solution)/shard_map/ppermute | solution.py:15
  54.7 4.6 %collective-permute-done.2 = f32[4,128,128]{2,0,1:T(4,128)S(1)} collective-permute-done((f32[4,128,128]{2,0,1:T(4,128)S(1)}, f32[4,128,128]{2,0,1:T(4,128)S(1)}, u32[]{:S(2)}, u32[]{:S(2)}) %collective-permute-start.2) | collective-permute-done | bytes 262176 | tf_op jit(solution)/shard_map/ppermute | solution.py:15
  59.5 1.3 collective-permute-start.5
  62.1 51.8 %collective-permute-done.5 = f32[4,128,128]{2,1,0:T(8,128)S(1)} collective-permute-done((f32[4,128,128]{2,1,0:T(8,128)S(1)}, f32[4,128,128]{2,1,0:T(8,128)S(1)}, u32[]{:S(2)}, u32[]{:S(2)}) %collective-permute-start.5) | collective-permute-done | bytes 262176 | tf_op jit(solution)/shard_map/ppermute | solution.py:15
  114.1 24.5 %while.37 = (s32[]{:T(128)}, f32[4,128,128]{2,0,1:T(4,128)S(1)}, f32[12,128,128]{2,0,1:T(8,128)S(1)}, s32[]{:T(128)}, s32[64]{0:T(128)S(1)}, /*index=5*/s32[]{:T...) while((s32[]{:T(128)}, f32[4,128,128]{2,0,1:T(4,128)S(1)}, ...), condition=%wide.region_3.4_spmd, body=%wide.region_2.3_spmd.sunk | while | flops 428083552 | bytes 8397583 | solution.py:50
  115.4 1.7 fusion.126
  118.7 2.1 fusion.127
  120.8 1.5 convolution_add_fusion.15
  123.6 1.7 fusion.126
  126.9 2.1 fusion.127
  128.9 1.5 convolution_add_fusion.15
  131.8 1.7 fusion.126
  135.0 2.1 fusion.127
  137.1 1.5 convolution_add_fusion.15
  138.7 1.3 collective-permute-start.7
  140.0 6.4 %collective-permute-start.6 = (f32[4,128,128]{2,0,1:T(4,128)S(1)}, f32[4,128,128]{2,0,1:T(4,128)S(1)}, u32[]{:S(2)}, u32[]{:S(2)}) collective-permute-start(f32[4,128,128]{2,0,1:T(4,128)S(1)} %get-tuple-element.250), channel_id=1, source_target_pairs={{0,4},{4,8},{8,12},{12,16},{16,20},{20,24},{24,28},{1,5},{5,9},{9,... | collective-permute-start | bytes 786440 | tf_op jit(solution)/shard_map/ppermute | solution.py:15
  146.5 3.8 collective-permute-done.6
  153.2 54.4 %collective-permute-done.9 = f32[4,128,128]{2,1,0:T(8,128)S(1)} collective-permute-done((f32[4,128,128]{2,1,0:T(8,128)S(1)}, f32[4,128,128]{2,1,0:T(8,128)S(1)}, u32[]{:S(2)}, u32[]{:S(2)}) %collective-permute-start.9) | collective-permute-done | bytes 262176 | tf_op jit(solution)/shard_map/ppermute | solution.py:15
  207.7 24.7 %while.38 = (s32[]{:T(128)}, f32[4,128,128]{2,0,1:T(4,128)S(1)}, f32[12,128,128]{2,0,1:T(8,128)S(1)}, s32[]{:T(128)}, s32[64]{0:T(128)S(1)}, /*index=5*/s32[]{:T...) while((s32[]{:T(128)}, f32[4,128,128]{2,0,1:T(4,128)S(1)}, ...), condition=%wide.region_5.6_spmd, body=%wide.region_4.5_spmd.sunk | while | flops 428083552 | bytes 8397583 | solution.py:50
  209.3 1.7 fusion.136
  212.5 2.1 fusion.137
  214.6 1.5 convolution_add_fusion.17
  217.4 1.7 fusion.136
  220.7 2.1 fusion.137
  222.8 1.5 convolution_add_fusion.17
  225.6 1.7 fusion.136
  228.9 2.1 fusion.137
  230.9 1.5 convolution_add_fusion.17
  232.5 1.3 collective-permute-start.11
  233.9 6.2 %collective-permute-start.10 = (f32[4,128,128]{2,0,1:T(4,128)S(1)}, f32[4,128,128]{2,0,1:T(4,128)S(1)}, u32[]{:S(2)}, u32[]{:S(2)}) collective-permute-start(f32[4,128,128]{2,0,1:T(4,128)S(1)} %get-tuple-element.248), channel_id=1, source_target_pairs={{0,4},{4,8},{8,12},{12,16},{16,20},{20,24},{24,28},{1,5},{5,9},{9,... | collective-permute-start | bytes 786440 | tf_op jit(solution)/shard_map/ppermute | solution.py:15
  240.1 3.8 collective-permute-done.10
  244.9 64.1 %all-gather.2.cloned.1.call-done = f32[512,512]{1,0:T(8,128)} async-done(((f32[512,128]{1,0:T(8,128)}), f32[512,512]{1,0:T(8,128)}) %all-gather.2.cloned.1.call-update) | async-done | bytes 1048592 | tf_op jit(solution)/shard_map/all_gather | solution.py:92
  308.9 2.8 convolution_multiply_fusion
  311.7 72.2 %all-reduce.2.cloned.1.call-done = f32[128,512]{1,0:T(8,128)} async-done(((f32[128,512]{1,0:T(8,128)}), f32[128,512]{1,0:T(8,128)}) %all-reduce.2.cloned.1.call-update) | async-done | bytes 262160 | tf_op jit(solution)/shard_map/psum | solution.py:102
  383.9 1.7 copy.69
  (106 shorter events, 35.2 us)
Async XLA Ops:
  7.2 301.8 %all-gather.2.cloned.1.call-start = ((), (), s32[]{:S(2)}) async-start(), calls=%async_computation | async-start | bytes 1310720 | tf_op jit(solution)/shard_map/all_gather | solution.py:92
  7.2 8.2 %copy-start.1 = (s32[64,2]{0,1:T(2,128)S(1)}, s32[64,2]{0,1:T(2,128)}, u32[]{:S(2)}) copy-start(s32[64,2]{0,1:T(2,128)} %param.12) | copy-start | bytes 1540
  7.2 14.9 %collective-permute-start.1 = (f32[4,128,128]{2,1,0:T(8,128)}, f32[4,128,128]{2,1,0:T(8,128)S(1)}, u32[]{:S(2)}, u32[]{:S(2)}) collective-permute-start(f32[4,128,128]{2,1,0:T(8,128)} %bitcast.89), channel_id=1, source_target_pairs={{8,0},{12,4},{16,8},{20,12},{24,16},{28,20},{9,1},{13,5},{17,9},{2... | collective-permute-start | bytes 786440 | tf_op jit(solution)/shard_map/ppermute | solution.py:15
  8.5 13.6 %collective-permute-start = (f32[4,128,128]{2,1,0:T(8,128)}, f32[4,128,128]{2,1,0:T(8,128)S(1)}, u32[]{:S(2)}, u32[]{:S(2)}) collective-permute-start(f32[4,128,128]{2,1,0:T(8,128)} %bitcast.90), channel_id=1, source_target_pairs={{4,0},{8,4},{12,8},{16,12},{20,16},{24,20},{28,24},{5,1},{9,5},{13... | collective-permute-start | bytes 786440 | tf_op jit(solution)/shard_map/ppermute | solution.py:15
  15.4 6.7 %copy-start = (f32[512,128]{1,0:T(8,128)S(1)}, f32[512,128]{1,0:T(8,128)}, u32[]{:S(2)}) copy-start(f32[512,128]{1,0:T(8,128)} %param.10) | copy-start | bytes 786436
  46.9 7.8 %collective-permute-start.3 = (f32[4,128,128]{2,0,1:T(4,128)S(1)}, f32[4,128,128]{2,0,1:T(4,128)S(1)}, u32[]{:S(2)}, u32[]{:S(2)}) collective-permute-start(f32[4,128,128]{2,0,1:T(4,128)S(1)} %get-tuple-element.253), channel_id=1, source_target_pairs={{0,8},{4,12},{8,16},{12,20},{16,24},{20,28},{1,9},{5,13},{9,17},{1... | collective-permute-start | bytes 786440 | tf_op jit(solution)/shard_map/ppermute | solution.py:15
  48.2 11.1 %collective-permute-start.2 = (f32[4,128,128]{2,0,1:T(4,128)S(1)}, f32[4,128,128]{2,0,1:T(4,128)S(1)}, u32[]{:S(2)}, u32[]{:S(2)}) collective-permute-start(f32[4,128,128]{2,0,1:T(4,128)S(1)} %get-tuple-element.252), channel_id=1, source_target_pairs={{0,4},{4,8},{8,12},{12,16},{16,20},{20,24},{24,28},{1,5},{5,9},{9,... | collective-permute-start | bytes 786440 | tf_op jit(solution)/shard_map/ppermute | solution.py:15
  59.5 54.4 %collective-permute-start.5 = (f32[4,128,128]{2,1,0:T(8,128)S(1)}, f32[4,128,128]{2,1,0:T(8,128)S(1)}, u32[]{:S(2)}, u32[]{:S(2)}) collective-permute-start(f32[4,128,128]{2,1,0:T(8,128)S(1)} %bitcast.83), channel_id=1, source_target_pairs={{8,0},{12,4},{16,8},{20,12},{24,16},{28,20},{9,1},{13,5},{17,9},{2... | collective-permute-start | bytes 786440 | tf_op jit(solution)/shard_map/ppermute | solution.py:15
  60.8 53.1 %collective-permute-start.4 = (f32[4,128,128]{2,1,0:T(8,128)S(1)}, f32[4,128,128]{2,1,0:T(8,128)S(1)}, u32[]{:S(2)}, u32[]{:S(2)}) collective-permute-start(f32[4,128,128]{2,1,0:T(8,128)S(1)} %bitcast.84), channel_id=1, source_target_pairs={{4,0},{8,4},{12,8},{16,12},{20,16},{24,20},{28,24},{5,1},{9,5},{13... | collective-permute-start | bytes 786440 | tf_op jit(solution)/shard_map/ppermute | solution.py:15
  138.7 7.8 %collective-permute-start.7 = (f32[4,128,128]{2,0,1:T(4,128)S(1)}, f32[4,128,128]{2,0,1:T(4,128)S(1)}, u32[]{:S(2)}, u32[]{:S(2)}) collective-permute-start(f32[4,128,128]{2,0,1:T(4,128)S(1)} %get-tuple-element.251), channel_id=1, source_target_pairs={{0,8},{4,12},{8,16},{12,20},{16,24},{20,28},{1,9},{5,13},{9,17},{1... | collective-permute-start | bytes 786440 | tf_op jit(solution)/shard_map/ppermute | solution.py:15
  140.0 10.3 %collective-permute-start.6 = (f32[4,128,128]{2,0,1:T(4,128)S(1)}, f32[4,128,128]{2,0,1:T(4,128)S(1)}, u32[]{:S(2)}, u32[]{:S(2)}) collective-permute-start(f32[4,128,128]{2,0,1:T(4,128)S(1)} %get-tuple-element.250), channel_id=1, source_target_pairs={{0,4},{4,8},{8,12},{12,16},{16,20},{20,24},{24,28},{1,5},{5,9},{9,... | collective-permute-start | bytes 786440 | tf_op jit(solution)/shard_map/ppermute | solution.py:15
  150.6 57.0 %collective-permute-start.9 = (f32[4,128,128]{2,1,0:T(8,128)S(1)}, f32[4,128,128]{2,1,0:T(8,128)S(1)}, u32[]{:S(2)}, u32[]{:S(2)}) collective-permute-start(f32[4,128,128]{2,1,0:T(8,128)S(1)} %bitcast.95), channel_id=1, source_target_pairs={{8,0},{12,4},{16,8},{20,12},{24,16},{28,20},{9,1},{13,5},{17,9},{2... | collective-permute-start | bytes 786440 | tf_op jit(solution)/shard_map/ppermute | solution.py:15
  151.9 55.7 %collective-permute-start.8 = (f32[4,128,128]{2,1,0:T(8,128)S(1)}, f32[4,128,128]{2,1,0:T(8,128)S(1)}, u32[]{:S(2)}, u32[]{:S(2)}) collective-permute-start(f32[4,128,128]{2,1,0:T(8,128)S(1)} %bitcast.96), channel_id=1, source_target_pairs={{4,0},{8,4},{12,8},{16,12},{20,16},{24,20},{28,24},{5,1},{9,5},{13... | collective-permute-start | bytes 786440 | tf_op jit(solution)/shard_map/ppermute | solution.py:15
  232.5 7.5 %collective-permute-start.11 = (f32[4,128,128]{2,0,1:T(4,128)S(1)}, f32[4,128,128]{2,0,1:T(4,128)S(1)}, u32[]{:S(2)}, u32[]{:S(2)}) collective-permute-start(f32[4,128,128]{2,0,1:T(4,128)S(1)} %get-tuple-element.249), channel_id=1, source_target_pairs={{0,8},{4,12},{8,16},{12,20},{16,24},{20,28},{1,9},{5,13},{9,17},{1... | collective-permute-start | bytes 786440 | tf_op jit(solution)/shard_map/ppermute | solution.py:15
  233.9 10.1 %collective-permute-start.10 = (f32[4,128,128]{2,0,1:T(4,128)S(1)}, f32[4,128,128]{2,0,1:T(4,128)S(1)}, u32[]{:S(2)}, u32[]{:S(2)}) collective-permute-start(f32[4,128,128]{2,0,1:T(4,128)S(1)} %get-tuple-element.248), channel_id=1, source_target_pairs={{0,4},{4,8},{8,12},{12,16},{16,20},{20,24},{24,28},{1,5},{5,9},{9,... | collective-permute-start | bytes 786440 | tf_op jit(solution)/shard_map/ppermute | solution.py:15
  244.8 139.1 %all-reduce.2.cloned.1.call-start = ((), (), s32[]{:S(2)}) async-start(), calls=%async_computation.1 | async-start | bytes 524288 | tf_op jit(solution)/shard_map/psum | solution.py:102
Sparse Core Ops, SparseCore 0:
  244.9 63.9 all-gather.1
  312.8 71.0 all-reduce.1
where the time goes:
time: 395 us; the launch traced here: 392 us
  waiting for transfers between devices  256 us (65%)
  matrix products  58.6 us (15%)
  starting transfers between devices  30 us (8%)
  local copies, waits for them, and re-layouts  18.4 us (5%)
  between operations  15 us (4%)
  other arithmetic  14 us (4%)
    ppermute x12, waiting for transfers between devices, from_behind(): return lax.ppermute(block, axis, route)  119 us
    psum x1, waiting for transfers between devices, shards(): gram = lax.psum(partial_block, 'domain')  72.2 us
    all_gather x1, waiting for transfers between devices, shards(): gathered = lax.all_gather(filtered, 'vec', axis=1, tiled=True)  64.1 us
    ppermute x12, starting transfers between devices, from_behind(): return lax.ppermute(block, axis, route)  29.9 us
    dot_general x9, matrix products, block_step(): jnp.einsum('tji,tjc->tic', tile, own[rloc], precision=lax.Precision.HIGHEST)  18.5 us
    dot_general x9, matrix products, block_step(): jnp.einsum('tij,tjc->tic', tile, window[cloc], precision=lax.Precision.HI...  15.2 us
    dot_general x9, matrix products, block_step(): jnp.einsum('tg,tic->gic', col_hot, back, precision=lax.Precision.HIGHEST)  13.5 us
    dot_general x9, matrix products, block_step(): jnp.einsum('tg,tic->gic', row_hot, fwd, precision=lax.Precision.HIGHEST)  8.57 us
  transfers between devices with their start and end apart: 14, of which 8 were waited for; matrix products, arithmetic and copies ran while one was open for 3% of the time, Pallas kernels for 0%

commit v1 on v0

--- a/solution.py
+++ b/solution.py
@@ -7,6 +7,12 @@
 REACH = 2
 center_shift = 1.0
 half_width = 1.5
+
+
+def add_all(x, axis):
+    parts = lax.all_gather(x, axis, axis=0, tiled=False)
+    total = parts.sum(axis=0)
+    return total
 
 
 def from_behind(block, axis, distance):
@@ -99,7 +105,7 @@
         )
         / total_rows
     )
-    gram = lax.psum(partial_block, "domain")
+    gram = add_all(partial_block, "domain")
     return (filtered, gram)
 
 

time: 395 us -> 373 us (0.944)
  waiting for transfers between devices: 256 us -> 233 us
    psum x1 -> x0, waiting for transfers between devices: 72.2 us -> none  [shards(): gram = lax.psum(partial_block, 'domain')]
    all_gather x0 -> x1, waiting for transfers between devices: none -> 49.2 us  [add_all(): parts = lax.all_gather(x, axis, axis=0, tiled=False)]
where the time goes in v1:
time: 373 us; the launch traced here: 370 us
  waiting for transfers between devices  233 us (62%)
  matrix products  58.6 us (16%)
  starting transfers between devices  30 us (8%)
  local copies, waits for them, and re-layouts  16.7 us (4%)
  other arithmetic  16.5 us (4%)
  between operations  15 us (4%)
    ppermute x12, waiting for transfers between devices, from_behind(): return lax.ppermute(block, axis, route)  119 us
    all_gather x1, waiting for transfers between devices, shards(): gathered = lax.all_gather(filtered, 'vec', axis=1, tiled=True)  64.1 us
    all_gather x1, waiting for transfers between devices, add_all(): parts = lax.all_gather(x, axis, axis=0, tiled=False)  49.2 us
    ppermute x12, starting transfers between devices, from_behind(): return lax.ppermute(block, axis, route)  29.9 us
    dot_general x9, matrix products, block_step(): jnp.einsum('tji,tjc->tic', tile, own[rloc], precision=lax.Precision.HIGHEST)  18.5 us
    dot_general x9, matrix products, block_step(): jnp.einsum('tij,tjc->tic', tile, window[cloc], precision=lax.Precision.HI...  15.2 us
    dot_general x9, matrix products, block_step(): jnp.einsum('tg,tic->gic', col_hot, back, precision=lax.Precision.HIGHEST)  13.5 us
    dot_general x9, matrix products, block_step(): jnp.einsum('tg,tic->gic', row_hot, fwd, precision=lax.Precision.HIGHEST)  8.57 us
  transfers between devices with their start and end apart: 14, of which 8 were waited for; matrix products, arithmetic and copies ran while one was open for 3% of the time, Pallas kernels for 0%

profile of v1, /device:TPU:0, one launch (start us, length us, event | category | flops | bytes accessed | tf_op | source)
XLA Modules:
  0.0 370.3 jit_solution(11295340561699356230)
XLA Ops:
  9.8 5.6 %copy.6 = f32[64,128,128]{1,2,0:T(8,128)} copy(f32[64,128,128]{2,1,0:T(8,128)} %param.11) | data formatting | bytes 8388608 | tf_op args[1]
  15.4 5.9 %fusion.61 = f32[64,128,128]{2,1,0:T(8,128)} fusion(f32[64,128,128]{2,1,0:T(8,128)} %param.11, f32[64,128,128]{1,2,0:T(8,128)} %copy.6, pred[64]{0:T(512)(128)(4,1)S(1)} %compare_bitcast_fusion), kind=kLoop, calls=%fused_computation.98 | loop fusion | flops 3145728 | bytes 12582976 | tf_op jit(solution)/shard_map/jit(_where)/select_n | solution.py:79
  22.3 24.5 %while.36 = (s32[]{:T(128)}, f32[4,128,128]{2,0,1:T(4,128)S(1)}, f32[12,128,128]{2,0,1:T(8,128)S(1)}, s32[]{:T(128)}, s32[64]{0:T(128)S(1)}, /*index=5*/s32[]{:T...) while((s32[]{:T(128)}, f32[4,128,128]{2,0,1:T(4,128)S(1)}, ...), condition=%wide.region_1.2_spmd, body=%wide.region_0.1_spmd.sunk | while | flops 428083552 | bytes 8397583 | solution.py:56
  23.6 1.7 fusion.116
  26.9 2.1 fusion.117
  29.0 1.5 convolution_add_fusion.13
  31.8 1.7 fusion.116
  35.1 2.1 fusion.117
  37.1 1.5 convolution_add_fusion.13
  40.0 1.7 fusion.116
  43.2 2.1 fusion.117
  45.3 1.5 convolution_add_fusion.13
  46.9 1.3 collective-permute-start.3
  48.2 5.6 %collective-permute-start.2 = (f32[4,128,128]{2,0,1:T(4,128)S(1)}, f32[4,128,128]{2,0,1:T(4,128)S(1)}, u32[]{:S(2)}, u32[]{:S(2)}) collective-permute-start(f32[4,128,128]{2,0,1:T(4,128)S(1)} %get-tuple-element.252), channel_id=1, source_target_pairs={{0,4},{4,8},{8,12},{12,16},{16,20},{20,24},{24,28},{1,5},{5,9},{9,... | collective-permute-start | bytes 786440 | tf_op jit(solution)/shard_map/ppermute | solution.py:21
  54.7 4.6 %collective-permute-done.2 = f32[4,128,128]{2,0,1:T(4,128)S(1)} collective-permute-done((f32[4,128,128]{2,0,1:T(4,128)S(1)}, f32[4,128,128]{2,0,1:T(4,128)S(1)}, u32[]{:S(2)}, u32[]{:S(2)}) %collective-permute-start.2) | collective-permute-done | bytes 262176 | tf_op jit(solution)/shard_map/ppermute | solution.py:21
  59.5 1.3 collective-permute-start.5
  62.1 51.8 %collective-permute-done.5 = f32[4,128,128]{2,1,0:T(8,128)S(1)} collective-permute-done((f32[4,128,128]{2,1,0:T(8,128)S(1)}, f32[4,128,128]{2,1,0:T(8,128)S(1)}, u32[]{:S(2)}, u32[]{:S(2)}) %collective-permute-start.5) | collective-permute-done | bytes 262176 | tf_op jit(solution)/shard_map/ppermute | solution.py:21
  114.1 24.5 %while.37 = (s32[]{:T(128)}, f32[4,128,128]{2,0,1:T(4,128)S(1)}, f32[12,128,128]{2,0,1:T(8,128)S(1)}, s32[]{:T(128)}, s32[64]{0:T(128)S(1)}, /*index=5*/s32[]{:T...) while((s32[]{:T(128)}, f32[4,128,128]{2,0,1:T(4,128)S(1)}, ...), condition=%wide.region_3.4_spmd, body=%wide.region_2.3_spmd.sunk | while | flops 428083552 | bytes 8397583 | solution.py:56
  115.4 1.7 fusion.126
  118.7 2.1 fusion.127
  120.8 1.5 convolution_add_fusion.15
  123.6 1.7 fusion.126
  126.9 2.1 fusion.127
  128.9 1.5 convolution_add_fusion.15
  131.8 1.7 fusion.126
  135.0 2.1 fusion.127
  137.1 1.5 convolution_add_fusion.15
  138.7 1.3 collective-permute-start.7
  140.0 6.4 %collective-permute-start.6 = (f32[4,128,128]{2,0,1:T(4,128)S(1)}, f32[4,128,128]{2,0,1:T(4,128)S(1)}, u32[]{:S(2)}, u32[]{:S(2)}) collective-permute-start(f32[4,128,128]{2,0,1:T(4,128)S(1)} %get-tuple-element.250), channel_id=1, source_target_pairs={{0,4},{4,8},{8,12},{12,16},{16,20},{20,24},{24,28},{1,5},{5,9},{9,... | collective-permute-start | bytes 786440 | tf_op jit(solution)/shard_map/ppermute | solution.py:21
  146.5 3.8 %collective-permute-done.6 = f32[4,128,128]{2,0,1:T(4,128)S(1)} collective-permute-done((f32[4,128,128]{2,0,1:T(4,128)S(1)}, f32[4,128,128]{2,0,1:T(4,128)S(1)}, u32[]{:S(2)}, u32[]{:S(2)}) %collective-permute-start.6) | collective-permute-done | bytes 262176 | tf_op jit(solution)/shard_map/ppermute | solution.py:21
  153.2 54.4 %collective-permute-done.9 = f32[4,128,128]{2,1,0:T(8,128)S(1)} collective-permute-done((f32[4,128,128]{2,1,0:T(8,128)S(1)}, f32[4,128,128]{2,1,0:T(8,128)S(1)}, u32[]{:S(2)}, u32[]{:S(2)}) %collective-permute-start.9) | collective-permute-done | bytes 262176 | tf_op jit(solution)/shard_map/ppermute | solution.py:21
  207.7 24.7 %while.38 = (s32[]{:T(128)}, f32[4,128,128]{2,0,1:T(4,128)S(1)}, f32[12,128,128]{2,0,1:T(8,128)S(1)}, s32[]{:T(128)}, s32[64]{0:T(128)S(1)}, /*index=5*/s32[]{:T...) while((s32[]{:T(128)}, f32[4,128,128]{2,0,1:T(4,128)S(1)}, ...), condition=%wide.region_5.6_spmd, body=%wide.region_4.5_spmd.sunk | while | flops 428083552 | bytes 8397583 | solution.py:56
  209.3 1.7 fusion.136
  212.5 2.1 fusion.137
  214.6 1.5 convolution_add_fusion.17
  217.4 1.7 fusion.136
  220.7 2.1 fusion.137
  222.8 1.5 convolution_add_fusion.17
  225.6 1.7 fusion.136
  228.9 2.1 fusion.137
  230.9 1.5 convolution_add_fusion.17
  232.5 1.3 collective-permute-start.11
  233.9 6.2 %collective-permute-start.10 = (f32[4,128,128]{2,0,1:T(4,128)S(1)}, f32[4,128,128]{2,0,1:T(4,128)S(1)}, u32[]{:S(2)}, u32[]{:S(2)}) collective-permute-start(f32[4,128,128]{2,0,1:T(4,128)S(1)} %get-tuple-element.248), channel_id=1, source_target_pairs={{0,4},{4,8},{8,12},{12,16},{16,20},{20,24},{24,28},{1,5},{5,9},{9,... | collective-permute-start | bytes 786440 | tf_op jit(solution)/shard_map/ppermute | solution.py:21
  240.1 3.8 %collective-permute-done.10 = f32[4,128,128]{2,0,1:T(4,128)S(1)} collective-permute-done((f32[4,128,128]{2,0,1:T(4,128)S(1)}, f32[4,128,128]{2,0,1:T(4,128)S(1)}, u32[]{:S(2)}, u32[]{:S(2)}) %collective-permute-start.10) | collective-permute-done | bytes 262176 | tf_op jit(solution)/shard_map/ppermute | solution.py:21
  244.9 64.1 %all-gather.4.cloned.1.call-done = f32[512,512]{1,0:T(8,128)} async-done(((f32[512,128]{1,0:T(8,128)}), f32[512,512]{1,0:T(8,128)}) %all-gather.4.cloned.1.call-update) | async-done | bytes 1048592 | tf_op jit(solution)/shard_map/all_gather | solution.py:98
  308.9 2.8 convolution_multiply_fusion
  311.7 49.2 %all-gather.6.cloned.1.call-done = f32[1024,512]{1,0:T(8,128)} async-done(((f32[128,512]{1,0:T(8,128)}), f32[1024,512]{1,0:T(8,128)}) %all-gather.6.cloned.1.call-update) | async-done | bytes 2097168 | tf_op jit(solution)/shard_map/all_gather | solution.py:13
  361.0 2.5 reduce_sum.9
  (106 shorter events, 35.2 us)
Async XLA Ops:
  7.2 301.8 %all-gather.4.cloned.1.call-start = ((), (), s32[]{:S(2)}) async-start(), calls=%async_computation | async-start | bytes 1310720 | tf_op jit(solution)/shard_map/all_gather | solution.py:98
  7.2 8.2 %copy-start.1 = (s32[64,2]{0,1:T(2,128)S(1)}, s32[64,2]{0,1:T(2,128)}, u32[]{:S(2)}) copy-start(s32[64,2]{0,1:T(2,128)} %param.12) | copy-start | bytes 1540
  7.2 14.9 %collective-permute-start.1 = (f32[4,128,128]{2,1,0:T(8,128)}, f32[4,128,128]{2,1,0:T(8,128)S(1)}, u32[]{:S(2)}, u32[]{:S(2)}) collective-permute-start(f32[4,128,128]{2,1,0:T(8,128)} %bitcast.90), channel_id=1, source_target_pairs={{8,0},{12,4},{16,8},{20,12},{24,16},{28,20},{9,1},{13,5},{17,9},{2... | collective-permute-start | bytes 786440 | tf_op jit(solution)/shard_map/ppermute | solution.py:21
  8.5 13.6 %collective-permute-start = (f32[4,128,128]{2,1,0:T(8,128)}, f32[4,128,128]{2,1,0:T(8,128)S(1)}, u32[]{:S(2)}, u32[]{:S(2)}) collective-permute-start(f32[4,128,128]{2,1,0:T(8,128)} %bitcast.91), channel_id=1, source_target_pairs={{4,0},{8,4},{12,8},{16,12},{20,16},{24,20},{28,24},{5,1},{9,5},{13... | collective-permute-start | bytes 786440 | tf_op jit(solution)/shard_map/ppermute | solution.py:21
  15.4 6.7 %copy-start = (f32[512,128]{1,0:T(8,128)S(1)}, f32[512,128]{1,0:T(8,128)}, u32[]{:S(2)}) copy-start(f32[512,128]{1,0:T(8,128)} %param.10) | copy-start | bytes 786436
  46.9 7.8 %collective-permute-start.3 = (f32[4,128,128]{2,0,1:T(4,128)S(1)}, f32[4,128,128]{2,0,1:T(4,128)S(1)}, u32[]{:S(2)}, u32[]{:S(2)}) collective-permute-start(f32[4,128,128]{2,0,1:T(4,128)S(1)} %get-tuple-element.253), channel_id=1, source_target_pairs={{0,8},{4,12},{8,16},{12,20},{16,24},{20,28},{1,9},{5,13},{9,17},{1... | collective-permute-start | bytes 786440 | tf_op jit(solution)/shard_map/ppermute | solution.py:21
  48.2 11.1 %collective-permute-start.2 = (f32[4,128,128]{2,0,1:T(4,128)S(1)}, f32[4,128,128]{2,0,1:T(4,128)S(1)}, u32[]{:S(2)}, u32[]{:S(2)}) collective-permute-start(f32[4,128,128]{2,0,1:T(4,128)S(1)} %get-tuple-element.252), channel_id=1, source_target_pairs={{0,4},{4,8},{8,12},{12,16},{16,20},{20,24},{24,28},{1,5},{5,9},{9,... | collective-permute-start | bytes 786440 | tf_op jit(solution)/shard_map/ppermute | solution.py:21
  59.5 54.4 %collective-permute-start.5 = (f32[4,128,128]{2,1,0:T(8,128)S(1)}, f32[4,128,128]{2,1,0:T(8,128)S(1)}, u32[]{:S(2)}, u32[]{:S(2)}) collective-permute-start(f32[4,128,128]{2,1,0:T(8,128)S(1)} %bitcast.84), channel_id=1, source_target_pairs={{8,0},{12,4},{16,8},{20,12},{24,16},{28,20},{9,1},{13,5},{17,9},{2... | collective-permute-start | bytes 786440 | tf_op jit(solution)/shard_map/ppermute | solution.py:21
  60.8 53.1 %collective-permute-start.4 = (f32[4,128,128]{2,1,0:T(8,128)S(1)}, f32[4,128,128]{2,1,0:T(8,128)S(1)}, u32[]{:S(2)}, u32[]{:S(2)}) collective-permute-start(f32[4,128,128]{2,1,0:T(8,128)S(1)} %bitcast.85), channel_id=1, source_target_pairs={{4,0},{8,4},{12,8},{16,12},{20,16},{24,20},{28,24},{5,1},{9,5},{13... | collective-permute-start | bytes 786440 | tf_op jit(solution)/shard_map/ppermute | solution.py:21
  138.7 7.8 %collective-permute-start.7 = (f32[4,128,128]{2,0,1:T(4,128)S(1)}, f32[4,128,128]{2,0,1:T(4,128)S(1)}, u32[]{:S(2)}, u32[]{:S(2)}) collective-permute-start(f32[4,128,128]{2,0,1:T(4,128)S(1)} %get-tuple-element.251), channel_id=1, source_target_pairs={{0,8},{4,12},{8,16},{12,20},{16,24},{20,28},{1,9},{5,13},{9,17},{1... | collective-permute-start | bytes 786440 | tf_op jit(solution)/shard_map/ppermute | solution.py:21
  140.0 10.3 %collective-permute-start.6 = (f32[4,128,128]{2,0,1:T(4,128)S(1)}, f32[4,128,128]{2,0,1:T(4,128)S(1)}, u32[]{:S(2)}, u32[]{:S(2)}) collective-permute-start(f32[4,128,128]{2,0,1:T(4,128)S(1)} %get-tuple-element.250), channel_id=1, source_target_pairs={{0,4},{4,8},{8,12},{12,16},{16,20},{20,24},{24,28},{1,5},{5,9},{9,... | collective-permute-start | bytes 786440 | tf_op jit(solution)/shard_map/ppermute | solution.py:21
  150.6 57.0 %collective-permute-start.9 = (f32[4,128,128]{2,1,0:T(8,128)S(1)}, f32[4,128,128]{2,1,0:T(8,128)S(1)}, u32[]{:S(2)}, u32[]{:S(2)}) collective-permute-start(f32[4,128,128]{2,1,0:T(8,128)S(1)} %bitcast.96), channel_id=1, source_target_pairs={{8,0},{12,4},{16,8},{20,12},{24,16},{28,20},{9,1},{13,5},{17,9},{2... | collective-permute-start | bytes 786440 | tf_op jit(solution)/shard_map/ppermute | solution.py:21
  151.9 55.7 %collective-permute-start.8 = (f32[4,128,128]{2,1,0:T(8,128)S(1)}, f32[4,128,128]{2,1,0:T(8,128)S(1)}, u32[]{:S(2)}, u32[]{:S(2)}) collective-permute-start(f32[4,128,128]{2,1,0:T(8,128)S(1)} %bitcast.97), channel_id=1, source_target_pairs={{4,0},{8,4},{12,8},{16,12},{20,16},{24,20},{28,24},{5,1},{9,5},{13... | collective-permute-start | bytes 786440 | tf_op jit(solution)/shard_map/ppermute | solution.py:21
  232.5 7.5 %collective-permute-start.11 = (f32[4,128,128]{2,0,1:T(4,128)S(1)}, f32[4,128,128]{2,0,1:T(4,128)S(1)}, u32[]{:S(2)}, u32[]{:S(2)}) collective-permute-start(f32[4,128,128]{2,0,1:T(4,128)S(1)} %get-tuple-element.249), channel_id=1, source_target_pairs={{0,8},{4,12},{8,16},{12,20},{16,24},{20,28},{1,9},{5,13},{9,17},{1... | collective-permute-start | bytes 786440 | tf_op jit(solution)/shard_map/ppermute | solution.py:21
  233.9 10.1 %collective-permute-start.10 = (f32[4,128,128]{2,0,1:T(4,128)S(1)}, f32[4,128,128]{2,0,1:T(4,128)S(1)}, u32[]{:S(2)}, u32[]{:S(2)}) collective-permute-start(f32[4,128,128]{2,0,1:T(4,128)S(1)} %get-tuple-element.248), channel_id=1, source_target_pairs={{0,4},{4,8},{8,12},{12,16},{16,20},{20,24},{24,28},{1,5},{5,9},{9,... | collective-permute-start | bytes 786440 | tf_op jit(solution)/shard_map/ppermute | solution.py:21
  244.8 116.2 %all-gather.6.cloned.1.call-start = ((), (), s32[]{:S(2)}) async-start(), calls=%async_computation.1 | async-start | bytes 2359296 | tf_op jit(solution)/shard_map/all_gather | solution.py:13
Sparse Core Ops, SparseCore 0:
  244.9 63.9 all-gather.3
  311.8 49.0 all-gather.5
